TPU v7x, 256 devices: a whole 4x4x8 slice. The times are simulated.
256 devices in a mesh: seq: 8 (over z_hi, x), exp: 32 (over z_lo, y, core).
Axes of the slice: x: 4, y: 4, z: 8 (z_hi: 2, z_lo: 4; z = z_hi * 4 + z_lo), core: 2. Of those that a mesh axis runs over, the one named last changes fastest.
Arguments:
- tokens: bfloat16 [8192, 1664], P('seq'), may hold values from -6 to 6
- out_grad: bfloat16 [8192, 1664], P('seq'), may hold values from -6 to 6
- slot_params: bfloat16 [1024, 1664], P('exp'), may hold values from -6 to 6
- first_mixing: float32 [64, 4, 4, 4], P('exp'), may hold values from -3 to 3
- first_blocks: bfloat16 [64, 4, 416, 2048], P('exp', None, None, 'seq'), may hold values from -0.15625 to 0.15625
- second_mixing: float32 [64, 4, 4, 4], P('exp'), may hold values from -3 to 3
- second_blocks: bfloat16 [64, 4, 2048, 416], P('exp', None, 'seq'), may hold values from -0.0625 to 0.0625
Outputs:
- grad_tokens: float32 [8192, 1664], P(('seq', 'exp'))
- grad_slots: float32 [1024, 1664], P('exp')
- grad_first_mixing: float32 [64, 4, 4, 4], P('exp')
- grad_first_blocks: bfloat16 [64, 4, 416, 2048], P('exp', None, None, 'seq')
- grad_second_mixing: float32 [64, 4, 4, 4], P('exp')
- grad_second_blocks: bfloat16 [64, 4, 2048, 416], P('exp', None, 'seq')
All inputs are finite; a program needn't handle non-finite values.
Results may differ from a plain program's by a relative error of at most 0.04.
Values may be sent and summed in bfloat16 or wider, within the bound.
No kernel may reach another device: no remote copies, remote signals or barrier semaphores. Data moves between devices by JAX's collectives and lax.ppermute only.
A program may use at most 128 MiB of HBM per device.

v0:
```python
import jax
import jax.numpy as jnp
from jax import lax
from jax.sharding import PartitionSpec as P

logit_gain = 64.0
norm_eps = 1e-06
gelu_coef = 0.7978845608028654
cubic_coef = 0.044715


def gelu_pair(preact):
    inner_arg = gelu_coef * (preact + cubic_coef * preact * preact * preact)
    tangent = jnp.tanh(inner_arg)
    output = 0.5 * preact * (1.0 + tangent)
    slopes = 0.5 * (1.0 + tangent) + 0.5 * preact * (1.0 - tangent * tangent) * gelu_coef * (
        1.0 + 3.0 * cubic_coef * preact * preact
    )
    return (output, slopes)


def mix_blocks(blocks, mixing):
    return jnp.einsum("sak,iab->sbik", blocks.astype(jnp.float32), mixing)


def expert_forward(slot_in, first_mixing, first_blocks, second_mixing, second_blocks):
    slots_here, model_width = slot_in.shape
    factors = first_mixing.shape[0]
    inner_width = model_width // factors
    hidden_block = first_blocks.shape[2]
    first_flat = (
        mix_blocks(slot_in.reshape(slots_here, factors, inner_width), first_mixing)
        .astype(jnp.bfloat16)
        .reshape(slots_here * factors, factors * inner_width)
    )
    preact = jnp.dot(
        first_flat,
        first_blocks.reshape(factors * inner_width, hidden_block),
        preferred_element_type=jnp.float32,
    ).reshape(slots_here, factors, hidden_block)
    activated, slopes = gelu_pair(preact)
    hidden = activated.astype(jnp.bfloat16)
    second_flat = (
        mix_blocks(hidden, second_mixing)
        .astype(jnp.bfloat16)
        .reshape(slots_here * factors, factors * hidden_block)
    )
    slot_out = jnp.dot(
        second_flat,
        second_blocks.reshape(factors * hidden_block, inner_width),
        preferred_element_type=jnp.float32,
    ).reshape(slots_here, model_width)
    return (slot_out, first_flat, hidden, slopes, second_flat)


def expert_backward(
    slot_in,
    grad_out,
    first_flat,
    hidden,
    slopes,
    second_flat,
    first_mixing,
    first_blocks,
    second_mixing,
    second_blocks,
):
    slots_here, model_width = slot_in.shape
    factors = first_mixing.shape[0]
    inner_width = model_width // factors
    hidden_block = first_blocks.shape[2]
    first_matrix = first_blocks.reshape(factors * inner_width, hidden_block)
    second_matrix = second_blocks.reshape(factors * hidden_block, inner_width)
    grad_rows = grad_out.reshape(slots_here * factors, inner_width)
    grad_second_in = jnp.dot(
        grad_rows, second_matrix.T, preferred_element_type=jnp.float32
    ).reshape(slots_here, factors, factors, hidden_block)
    grad_second_blocks = (
        jnp.dot(second_flat.T, grad_rows, preferred_element_type=jnp.float32)
        .astype(jnp.bfloat16)
        .reshape(factors, hidden_block, inner_width)
    )
    grad_second_mixing = jnp.einsum("sak,sbik->iab", hidden.astype(jnp.float32), grad_second_in)
    grad_hidden = jnp.einsum("iab,sbik->sak", second_mixing, grad_second_in)
    grad_preact = (
        (grad_hidden * slopes).astype(jnp.bfloat16).reshape(slots_here * factors, hidden_block)
    )
    grad_first_in = jnp.dot(
        grad_preact, first_matrix.T, preferred_element_type=jnp.float32
    ).reshape(slots_here, factors, factors, inner_width)
    grad_first_blocks = (
        jnp.dot(first_flat.T, grad_preact, preferred_element_type=jnp.float32)
        .astype(jnp.bfloat16)
        .reshape(factors, inner_width, hidden_block)
    )
    slot_split = slot_in.reshape(slots_here, factors, inner_width).astype(jnp.float32)
    grad_first_mixing = jnp.einsum("sad,sbid->iab", slot_split, grad_first_in)
    grad_slot = jnp.einsum("iab,sbid->sad", first_mixing, grad_first_in).reshape(
        slots_here, model_width
    )
    return (grad_slot, grad_first_mixing, grad_first_blocks, grad_second_mixing, grad_second_blocks)


def token_total(partial_sums):
    return lax.psum(partial_sums, "exp")


def slot_total(first_part, second_part):
    return lax.psum((first_part, second_part), "seq")


def unit_grad(unit_rows, unit_grad_rows, norms):
    return (
        unit_grad_rows - unit_rows * jnp.sum(unit_rows * unit_grad_rows, axis=1, keepdims=True)
    ) / norms


def local(tokens, out_grad, slot_params, first_mixing, first_blocks, second_mixing, second_blocks):
    token_values = tokens.astype(jnp.float32)
    token_norm = jnp.sqrt(jnp.sum(token_values * token_values, axis=1, keepdims=True) + norm_eps)
    token_unit = token_values / token_norm
    token_unit_b = token_unit.astype(jnp.bfloat16)
    slot_values = slot_params.astype(jnp.float32)
    slot_norm = jnp.sqrt(jnp.sum(slot_values * slot_values, axis=1, keepdims=True) + norm_eps)
    slot_unit = slot_values / slot_norm
    slot_unit_b = slot_unit.astype(jnp.bfloat16)
    logits = logit_gain * jnp.einsum(
        "sd,td->st", slot_unit_b, token_unit_b, preferred_element_type=jnp.float32
    )
    weights = jnp.exp(logits)
    input_part = jnp.dot(weights.astype(jnp.bfloat16), tokens, preferred_element_type=jnp.float32)
    combine_total = token_total(jnp.sum(weights, axis=0))
    input_sum, dispatch_total = slot_total(input_part, jnp.sum(weights, axis=1))
    slot_inputs = input_sum / dispatch_total[:, None]
    slot_inputs_b = slot_inputs.astype(jnp.bfloat16)
    dispatch = weights / dispatch_total[:, None]
    combine = weights / combine_total[None, :]
    grad_out_part = jnp.dot(
        combine.astype(jnp.bfloat16), out_grad, preferred_element_type=jnp.float32
    )
    experts_here = first_mixing.shape[0]
    model_width = tokens.shape[1]
    slots_each = slot_inputs_b.shape[0] // experts_here
    grouped = slot_inputs_b.reshape(experts_here, slots_each, model_width)
    slot_out_part, first_flat, hidden, slopes, second_flat = jax.vmap(expert_forward)(
        grouped, first_mixing, first_blocks, second_mixing, second_blocks
    )
    slot_out_sum, slot_grad_sum = slot_total(
        slot_out_part.reshape(experts_here * slots_each, model_width), grad_out_part
    )
    slot_out_b = slot_out_sum.astype(jnp.bfloat16)
    slot_grad_b = slot_grad_sum.astype(jnp.bfloat16)
    combine_grad = jnp.einsum("sd,td->st", slot_out_b, out_grad, preferred_element_type=jnp.float32)
    combine_dot = token_total(jnp.sum(combine * combine_grad, axis=0))
    expert_results = jax.vmap(expert_backward)(
        grouped,
        slot_grad_b.reshape(experts_here, slots_each, model_width),
        first_flat,
        hidden,
        slopes,
        second_flat,
        first_mixing,
        first_blocks,
        second_mixing,
        second_blocks,
    )
    input_grad_part, first_mix_part, first_blocks_grad, second_mix_part, second_blocks_grad = (
        expert_results
    )
    input_grad, mixing_grads = slot_total(
        input_grad_part.reshape(experts_here * slots_each, model_width),
        jnp.stack([first_mix_part, second_mix_part]),
    )
    input_grad_b = input_grad.astype(jnp.bfloat16)
    dispatch_dot = jnp.sum(slot_inputs * input_grad, axis=1)
    dispatch_grad = jnp.einsum(
        "sd,td->st", input_grad_b, tokens, preferred_element_type=jnp.float32
    )
    logit_grad = combine * (combine_grad - combine_dot[None, :]) + dispatch * (
        dispatch_grad - dispatch_dot[:, None]
    )
    logit_grad_b = (logit_gain * logit_grad).astype(jnp.bfloat16)
    slot_unit_grad = lax.psum(
        jnp.dot(logit_grad_b, token_unit_b, preferred_element_type=jnp.float32), "seq"
    )
    grad_slots = unit_grad(slot_unit, slot_unit_grad, slot_norm)
    row_count = tokens.shape[0] // lax.axis_size("exp")
    grad_all, out_all, unit_all = (
        lax.all_gather(input_grad_b, "exp", axis=0, tiled=True),
        lax.all_gather(slot_out_b, "exp", axis=0, tiled=True),
        lax.all_gather(slot_unit_b, "exp", axis=0, tiled=True),
    )
    dispatch_all, dot_all = (
        lax.all_gather(dispatch_total, "exp", axis=0, tiled=True),
        lax.all_gather(dispatch_dot, "exp", axis=0, tiled=True),
    )
    first_row = lax.axis_index("exp") * row_count
    own_tokens = lax.dynamic_slice_in_dim(tokens, first_row, row_count, 0)
    own_grad = lax.dynamic_slice_in_dim(out_grad, first_row, row_count, 0)
    own_unit = lax.dynamic_slice_in_dim(token_unit, first_row, row_count, 0)
    own_unit_b = lax.dynamic_slice_in_dim(token_unit_b, first_row, row_count, 0)
    own_norm = lax.dynamic_slice_in_dim(token_norm, first_row, row_count, 0)
    own_total = lax.dynamic_slice_in_dim(combine_total, first_row, row_count, 0)
    own_dot = lax.dynamic_slice_in_dim(combine_dot, first_row, row_count, 0)
    own_weights = jnp.exp(
        logit_gain * jnp.dot(own_unit_b, unit_all.T, preferred_element_type=jnp.float32)
    )
    own_dispatch = own_weights / dispatch_all[None, :]
    own_combine = own_weights / own_total[:, None]
    own_combine_grad = jnp.dot(own_grad, out_all.T, preferred_element_type=jnp.float32)
    own_dispatch_grad = jnp.dot(own_tokens, grad_all.T, preferred_element_type=jnp.float32)
    own_logit = own_combine * (own_combine_grad - own_dot[:, None]) + own_dispatch * (
        own_dispatch_grad - dot_all[None, :]
    )
    own_logit_b = (logit_gain * own_logit).astype(jnp.bfloat16)
    direct = jnp.dot(
        own_dispatch.astype(jnp.bfloat16), grad_all, preferred_element_type=jnp.float32
    )
    through = jnp.dot(own_logit_b, unit_all, preferred_element_type=jnp.float32)
    grad_tokens = direct + unit_grad(own_unit, through, own_norm)
    return (
        grad_tokens,
        grad_slots,
        mixing_grads[0],
        first_blocks_grad,
        mixing_grads[1],
        second_blocks_grad,
    )


def solution(mesh):
    placed = (
        P("seq", None),
        P("seq", None),
        P("exp", None),
        P("exp", None, None, None),
        P("exp", None, None, "seq"),
        P("exp", None, None, None),
        P("exp", None, "seq", None),
    )
    return jax.shard_map(
        local,
        mesh=mesh,
        in_specs=placed,
        out_specs=(
            P(("seq", "exp"), None),
            P("exp", None),
            P("exp", None, None, None),
            P("exp", None, None, "seq"),
            P("exp", None, None, None),
            P("exp", None, "seq", None),
        ),
        check_vma=False,
    )
```

profile of v0, /device:TPU:1, one launch (start us, length us, event | category | flops | bytes accessed | tf_op | source)
XLA Modules:
  0.0 651.7 jit_solution(12688127571988477652)
XLA Ops:
  8.1 2.9 fusion
  11.2 5.0 convert_divide_fusion
  17.6 3.9 fusion.57
  23.0 71.5 %psum.64 = f32[1024]{0:T(1024)S(1)} all-reduce(f32[1024]{0:T(1024)S(1)} %get-tuple-element.19), channel_id=1, replica_groups=mesh['seq'=8,'exp'=32] {'exp'}, use_global_device_ids=true, to_apply=%region_5.0 | all-reduce | flops 1024 | bytes 8192 | tf_op jit(solution)/shard_map/psum | solution.py:105
  96.5 50.3 %all-reduce.16 = (bf16[32,1664]{1,0:T(8,128)(2,1)}, f32[32]{0:T(128)}) all-reduce(f32[32,1664]{1,0:T(8,128)} %fusion.41, f32[32]{0:T(128)} %get-tuple-element.18), channel_id=1, replica_groups=mesh['seq'=8,'exp'=32] {'seq'}, use_global_device_ids=true, to_apply=%region_6.0 | all-reduce | flops 53280 | bytes 319744 | tf_op jit(solution)/shard_map/psum | solution.py:109
  152.5 1.8 reshape.84
  166.3 2.3 reshape.85
  168.6 2.7 fusion.67
  172.8 2.0 fusion.2
  174.8 1.9 convolution_bitcast_fusion.3
  176.7 2.0 fusion.15
  180.2 2.9 fusion.68
  183.0 2.5 reshape.89
  185.6 2.2 convolution_bitcast_fusion.2
  191.8 1.8 reshape.91
  193.6 2.9 fusion.69
  198.3 2.2 convolution_bitcast_fusion
  200.4 1.9 reshape.90
  203.7 46.9 %all-reduce.17 = (bf16[32,1664]{1,0:T(8,128)(2,1)}, f32[2,2,4,4,4]{4,3,2,1,0:T(4,128)}) all-reduce(f32[32,1664]{1,0:T(8,128)} %reshape.92, f32[2,2,4,4,4]{4,3,2,1,0:T(4,128)} %pad_maximum_fusion), channel_id=1, replica_groups=mesh['seq'=8,'exp'=32] {'seq'}, use_global_device_ids=true, to_apply=%region_9.0 | all-reduce | flops 53504 | bytes 321536 | tf_op jit(solution)/shard_map/psum | solution.py:109
  250.7 3.2 multiply_reduce_fusion.3
  253.9 51.0 %all-reduce.13.cloned.1.call-done = f32[32,1664]{1,0:T(8,128)} async-done(((f32[32,1664]{1,0:T(8,128)}), f32[32,1664]{1,0:T(8,128)}) %all-reduce.13.cloned.1.call-update) | async-done | bytes 213008 | tf_op jit(solution)/shard_map/psum | solution.py:109
  304.9 1.9 multiply_reduce_fusion.2
  307.3 132.5 %all-reduce.2 = (f32[1024]{0:T(1024)}, f32[1024]{0:T(1024)}, f32[1024]{0:T(1024)S(1)}) all-reduce(f32[1024]{0:T(1024)} %get-tuple-element.34, f32[1024]{0:T(1024)S(1)} %dynamic-update-slice.1, f32[1024]{0:T(1024)S(1)} %copy-done.14), channel_id=1, replica_groups=mesh['seq'=8,'exp'=32] {'exp'}, use_global_device_ids=true, to_apply=%region_11.0 | all-reduce | flops 3072 | bytes 24576 | tf_op jit(solution)/shard_map/psum | solution.py:105
  439.8 5.5 fusion.16
  451.6 1.8 convolution_convert_fusion
  454.7 89.4 %all-reduce.15.cloned.1.call-done = f32[32,1664]{1,0:T(8,128)} async-done(((f32[32,1664]{1,0:T(8,128)}), f32[32,1664]{1,0:T(8,128)}) %all-reduce.15.cloned.1.call-update) | async-done | bytes 213008 | tf_op jit(solution)/shard_map/psum | solution.py:183
  547.0 3.2 fusion.12
  550.2 22.4 %all-gather.8.cloned.1.call-done = bf16[1024,1664]{1,0:T(8,128)(2,1)} async-done(((bf16[32,1664]{1,0:T(8,128)(2,1)}), bf16[1024,1664]{1,0:T(8,128)(2,1)}) %all-gather.8.cloned.1.call-update) | async-done | bytes 3407888 | tf_op jit(solution)/shard_map/all_gather | solution.py:190
  572.6 3.7 fusion.10
  576.3 59.0 %all-gather.6.cloned.1.call-done = bf16[1024,1664]{1,0:T(8,128)(2,1)} async-done(((bf16[32,1664]{1,0:T(8,128)(2,1)}), bf16[1024,1664]{1,0:T(8,128)(2,1)}) %all-gather.6.cloned.1.call-update) | async-done | bytes 3407888 | tf_op jit(solution)/shard_map/all_gather | solution.py:189
  635.3 5.5 multiply_reduce_fusion.1
  640.8 3.5 convolution_add_fusion
  (91 shorter events, 43.3 us)
Async XLA Ops:
  8.0 87.1 %copy-start = (bf16[1024,1664]{1,0:T(8,128)(2,1)S(1)}, bf16[1024,1664]{1,0:T(8,128)(2,1)}, u32[]{:S(2)}) copy-start(bf16[1024,1664]{1,0:T(8,128)(2,1)} %param.8) | copy-start | bytes 10223620
  8.0 152.4 %all-reduce.11.cloned.1.call-start = ((), (), s32[]{:S(2)}) async-start(), calls=%async_computation.1 | async-start | bytes 425984 | tf_op jit(solution)/shard_map/psum | solution.py:109
  8.1 3.1 copy-start.1
  11.2 5.0 copy-start.13
  11.2 5.0 copy-start.5
  16.3 0.6 copy-start.16
  17.6 3.9 copy-start.2
  23.0 282.0 %all-reduce.13.cloned.1.call-start = ((), (), s32[]{:S(2)}) async-start(), calls=%async_computation.2 | async-start | bytes 425984 | tf_op jit(solution)/shard_map/psum | solution.py:109
  94.5 0.6 copy-start.10
  96.5 59.4 %copy-start.9 = (f32[2,4,4,4]{3,2,1,0:T(4,128)S(1)}, f32[2,4,4,4]{3,2,1,0:T(4,128)}, u32[]{:S(2)}) copy-start(f32[2,4,4,4]{3,2,1,0:T(4,128)} %param.10) | copy-start | bytes 1540
  148.5 2.9 copy-start.7
  150.2 1.2 copy-start.3
  165.2 7.6 %copy-start.15 = (f32[2,4,4,4]{3,2,1,0:T(4,128)S(1)}, f32[2,4,4,4]{3,2,1,0:T(4,128)}, u32[]{:S(2)}) copy-start(f32[2,4,4,4]{3,2,1,0:T(4,128)} %param.12) | copy-start | bytes 1540
  202.3 341.8 %all-reduce.15.cloned.1.call-start = ((), (), s32[]{:S(2)}) async-start(), calls=%async_computation.5 | async-start | bytes 425984 | tf_op jit(solution)/shard_map/psum | solution.py:183
  203.7 101.2 %copy-start.18 = (f32[32]{0:T(128)S(1)}, f32[32]{0:T(128)}, u32[]{:S(2)}) copy-start(f32[32]{0:T(128)} %get-tuple-element.26) | copy-start | bytes 388
  203.7 103.6 %copy-start.14 = (f32[1024]{0:T(1024)S(1)}, f32[1024]{0:T(1024)}, u32[]{:S(2)}) copy-start(f32[1024]{0:T(1024)} %dynamic-update-slice) | copy-start | bytes 12292
  203.7 236.1 %copy-start.11 = (f32[1024]{0:T(1024)S(1)}, f32[1024]{0:T(1024)}, u32[]{:S(2)}) copy-start(f32[1024]{0:T(1024)} %copy-done.10) | copy-start | bytes 12292
  306.8 0.5 copy-start.20
  445.3 101.7 %all-gather.4.cloned.1.call-start = ((), (), s32[]{:S(2)}) async-start(), calls=%async_computation | async-start | bytes 3514368 | tf_op jit(solution)/shard_map/all_gather | solution.py:191
  445.9 126.6 %all-gather.8.cloned.1.call-start = ((), (), s32[]{:S(2)}) async-start(), calls=%async_computation.4 | async-start | bytes 3514368 | tf_op jit(solution)/shard_map/all_gather | solution.py:190
  446.5 188.8 %all-gather.6.cloned.1.call-start = ((), (), s32[]{:S(2)}) async-start(), calls=%async_computation.3 | async-start | bytes 3514368 | tf_op jit(solution)/shard_map/all_gather | solution.py:189
  447.1 3.9 copy-start.12
  447.1 4.5 copy-start.4
  447.1 4.5 copy-start.8
  448.0 96.1 %copy-start.6 = (bf16[32,1664]{1,0:T(8,128)(2,1)S(1)}, bf16[32,1664]{1,0:T(8,128)(2,1)}, u32[]{:S(2)}) copy-start(bf16[32,1664]{1,0:T(8,128)(2,1)} %param.9) | copy-start | bytes 319492
  448.0 96.1 %copy-start.17 = (f32[32]{0:T(128)S(1)}, f32[32]{0:T(128)}, u32[]{:S(2)}) copy-start(f32[32]{0:T(128)} %copy-done.16) | copy-start | bytes 388
  547.0 88.3 %copy-start.19 = (f32[1024]{0:T(1024)S(1)}, f32[1024]{0:T(1024)}, u32[]{:S(2)}) copy-start(f32[1024]{0:T(1024)} %get-tuple-element.21) | copy-start | bytes 12292
Sparse Core Ops, SparseCore 0:
  23.1 102.7 all-reduce.10
  202.4 102.4 all-reduce.12
  445.5 98.6 all-reduce.14
Sparse Core Ops, SparseCore 1:
  447.7 62.2 all-gather.3
  511.8 60.7 all-gather.7
  574.3 61.0 all-gather.5
where the time goes:
time: 653 us; the launch traced here: 652 us
  blocking collectives  301 us (46%)
  waiting for transfers between devices  223 us (34%)
  matrix products  55.9 us (9%)
  local copies, waits for them, and re-layouts  38.1 us (6%)
  other arithmetic  16.5 us (3%)
  between operations  16.3 us (2%)
    psum x2, blocking collectives, token_total(): return lax.psum(partial_sums, 'exp')  204 us
    psum x2, blocking collectives, slot_total(): return lax.psum((first_part, second_part), 'seq')  97.3 us
    psum x1, waiting for transfers between devices, local(): lax.psum(jnp.dot(logit_grad_b, token_unit_b, preferred_element_type=jnp.f...  89.4 us
    all_gather x1, waiting for transfers between devices, local(): lax.all_gather(input_grad_b, 'exp', axis=0, tiled=True)  59 us
    psum x2, waiting for transfers between devices, slot_total(): return lax.psum((first_part, second_part), 'seq')  51 us
    all_gather x1, waiting for transfers between devices, local(): lax.all_gather(slot_out_b, 'exp', axis=0, tiled=True)  22.4 us
  transfers between devices with their start and end apart: 6, of which 4 were waited for; matrix products, arithmetic and copies ran while one was open for 5% of the time, Pallas kernels for 0%

commit v1 on v0

--- a/solution.py
+++ b/solution.py
@@ -186,7 +186,9 @@
     grad_slots = unit_grad(slot_unit, slot_unit_grad, slot_norm)
     row_count = tokens.shape[0] // lax.axis_size("exp")
     grad_all, out_all, unit_all = (
-        lax.all_gather(input_grad_b, "exp", axis=0, tiled=True),
+        jnp.concatenate(
+            lax.all_to_all(jnp.stack([input_grad_b] * lax.axis_size("exp")), "exp", 0, 0), axis=0
+        ),
         lax.all_gather(slot_out_b, "exp", axis=0, tiled=True),
         lax.all_gather(slot_unit_b, "exp", axis=0, tiled=True),
     )

time: 653 us -> 633 us (0.969)
  waiting for transfers between devices: 223 us -> 189 us
  starting transfers between devices: 0.25 us -> 10.9 us
    all_gather x1 -> x0, waiting for transfers between devices: 59 us -> none  [local(): lax.all_gather(input_grad_b, 'exp', axis=0, tiled=True)]
    psum x1, waiting for transfers between devices: 89.4 us -> 102 us  [local(): lax.psum(jnp.dot(logit_grad_b, token_unit_b, preferred_element_type=jnp.f...]
    all_gather x1, waiting for transfers between devices: 22.4 us -> 34.3 us  [local(): lax.all_gather(slot_out_b, 'exp', axis=0, tiled=True)]
    all_to_all x0 -> x1, starting transfers between devices: none -> 10.7 us  [local(): lax.all_to_all(jnp.stack([input_grad_b] * lax.axis_size('exp')), 'exp', 0...]
  transfers between devices with their start and end apart: 6 -> 6, of which waited for: 4 -> 3; matrix products, arithmetic and copies ran while one was open for 5% -> 6% of each run, Pallas kernels for 0% -> 0%
where the time goes in v1:
time: 633 us; the launch traced here: 631 us
  blocking collectives  300 us (47%)
  waiting for transfers between devices  189 us (30%)
  matrix products  56.8 us (9%)
  local copies, waits for them, and re-layouts  41.6 us (7%)
  other arithmetic  16.5 us (3%)
  between operations  16 us (3%)
  starting transfers between devices  10.9 us (2%)
    psum x2, blocking collectives, token_total(): return lax.psum(partial_sums, 'exp')  204 us
    psum x1, waiting for transfers between devices, local(): lax.psum(jnp.dot(logit_grad_b, token_unit_b, preferred_element_type=jnp.f...  102 us
    psum x2, blocking collectives, slot_total(): return lax.psum((first_part, second_part), 'seq')  96.3 us
    psum x2, waiting for transfers between devices, slot_total(): return lax.psum((first_part, second_part), 'seq')  51.7 us
    all_gather x1, waiting for transfers between devices, local(): lax.all_gather(slot_out_b, 'exp', axis=0, tiled=True)  34.3 us
  transfers between devices with their start and end apart: 6, of which 3 were waited for; matrix products, arithmetic and copies ran while one was open for 6% of the time, Pallas kernels for 0%

profile of v1, /device:TPU:1, one launch (start us, length us, event | category | flops | bytes accessed | tf_op | source)
XLA Modules:
  0.0 631.2 jit_solution(11375840291696572850)
XLA Ops:
  8.1 2.9 fusion
  11.2 5.0 convert_divide_fusion
  17.5 3.9 fusion.57
  22.9 71.5 %psum.64 = f32[1024]{0:T(1024)S(1)} all-reduce(f32[1024]{0:T(1024)S(1)} %get-tuple-element.19), channel_id=1, replica_groups=mesh['seq'=8,'exp'=32] {'exp'}, use_global_device_ids=true, to_apply=%region_5.0 | all-reduce | flops 1024 | bytes 8192 | tf_op jit(solution)/shard_map/psum | solution.py:105
  96.4 50.6 %all-reduce.16 = (bf16[32,1664]{1,0:T(8,128)(2,1)}, f32[32]{0:T(128)}) all-reduce(f32[32,1664]{1,0:T(8,128)} %fusion.41, f32[32]{0:T(128)} %get-tuple-element.18), channel_id=1, replica_groups=mesh['seq'=8,'exp'=32] {'seq'}, use_global_device_ids=true, to_apply=%region_6.0 | all-reduce | flops 53280 | bytes 319744 | tf_op jit(solution)/shard_map/psum | solution.py:109
  152.7 1.8 reshape.89
  166.5 2.3 reshape.90
  168.8 2.7 fusion.67
  173.0 2.0 fusion.2
  175.0 1.9 convolution_bitcast_fusion.3
  176.9 2.0 fusion.15
  180.4 2.9 fusion.68
  183.3 2.5 reshape.94
  185.8 2.2 convolution_bitcast_fusion.2
  193.8 2.9 fusion.69
  198.5 2.2 convolution_bitcast_fusion
  200.7 1.9 reshape.95
  204.0 45.7 %all-reduce.17 = (bf16[32,1664]{1,0:T(8,128)(2,1)}, f32[2,2,4,4,4]{4,3,2,1,0:T(4,128)}) all-reduce(f32[32,1664]{1,0:T(8,128)} %reshape.98, f32[2,2,4,4,4]{4,3,2,1,0:T(4,128)} %pad_maximum_fusion), channel_id=1, replica_groups=mesh['seq'=8,'exp'=32] {'seq'}, use_global_device_ids=true, to_apply=%region_9.0 | all-reduce | flops 53504 | bytes 321536 | tf_op jit(solution)/shard_map/psum | solution.py:109
  249.6 3.3 multiply_reduce_fusion.3
  252.9 51.7 %all-reduce.13.cloned.1.call-done = f32[32,1664]{1,0:T(8,128)} async-done(((f32[32,1664]{1,0:T(8,128)}), f32[32,1664]{1,0:T(8,128)}) %all-reduce.13.cloned.1.call-update) | async-done | bytes 213008 | tf_op jit(solution)/shard_map/psum | solution.py:109
  304.6 1.9 multiply_reduce_fusion.2
  307.0 132.5 %all-reduce.2 = (f32[1024]{0:T(1024)}, f32[1024]{0:T(1024)}, f32[1024]{0:T(1024)S(1)}) all-reduce(f32[1024]{0:T(1024)} %get-tuple-element.34, f32[1024]{0:T(1024)S(1)} %dynamic-update-slice.1, f32[1024]{0:T(1024)S(1)} %copy-done.12), channel_id=1, replica_groups=mesh['seq'=8,'exp'=32] {'exp'}, use_global_device_ids=true, to_apply=%region_11.0 | all-reduce | flops 3072 | bytes 24576 | tf_op jit(solution)/shard_map/psum | solution.py:105
  439.5 5.5 fusion.16
  446.2 2.9 stack.8
  449.0 10.7 %all-to-all-start = ((bf16[32,32,1664]{2,1,0:T(8,128)(2,1)}), bf16[32,32,1664]{2,1,0:T(8,128)(2,1)}, u32[]{:S(2)}, u32[]{:S(2)}) async-start(bf16[32,32,1664]{2,1,0:T(8,128)(2,1)} %stack.8), calls=%async_computation | async-start | bytes 6815744 | tf_op jit(solution)/shard_map/all_to_all | solution.py:190
  464.9 2.7 convolution_convert_fusion
  468.9 102.1 %all-reduce.15.cloned.1.call-done = f32[32,1664]{1,0:T(8,128)} async-done(((f32[32,1664]{1,0:T(8,128)}), f32[32,1664]{1,0:T(8,128)}) %all-reduce.15.cloned.1.call-update) | async-done | bytes 213008 | tf_op jit(solution)/shard_map/psum | solution.py:183
  573.9 3.1 fusion.12
  577.1 34.3 %all-gather.5.cloned.1.call-done = bf16[1024,1664]{1,0:T(8,128)(2,1)} async-done(((bf16[32,1664]{1,0:T(8,128)(2,1)}), bf16[1024,1664]{1,0:T(8,128)(2,1)}) %all-gather.5.cloned.1.call-update) | async-done | bytes 3407888 | tf_op jit(solution)/shard_map/all_gather | solution.py:192
  611.3 3.7 fusion.10
  615.1 5.5 multiply_reduce_fusion.1
  620.6 3.5 convolution_add_fusion
  (87 shorter events, 45.2 us)
Async XLA Ops:
  8.0 87.0 %copy-start = (bf16[1024,1664]{1,0:T(8,128)(2,1)S(1)}, bf16[1024,1664]{1,0:T(8,128)(2,1)}, u32[]{:S(2)}) copy-start(bf16[1024,1664]{1,0:T(8,128)(2,1)} %param.8) | copy-start | bytes 10223620
  8.0 152.6 %all-reduce.11.cloned.1.call-start = ((), (), s32[]{:S(2)}) async-start(), calls=%async_computation.2 | async-start | bytes 425984 | tf_op jit(solution)/shard_map/psum | solution.py:109
  8.1 3.1 copy-start.1
  11.2 5.0 copy-start.11
  11.2 5.0 copy-start.5
  16.3 0.5 copy-start.14
  17.5 3.9 copy-start.2
  22.9 281.7 %all-reduce.13.cloned.1.call-start = ((), (), s32[]{:S(2)}) async-start(), calls=%async_computation.3 | async-start | bytes 425984 | tf_op jit(solution)/shard_map/psum | solution.py:109
  94.4 0.6 copy-start.9
  96.4 59.7 %copy-start.8 = (f32[2,4,4,4]{3,2,1,0:T(4,128)S(1)}, f32[2,4,4,4]{3,2,1,0:T(4,128)}, u32[]{:S(2)}) copy-start(f32[2,4,4,4]{3,2,1,0:T(4,128)} %param.10) | copy-start | bytes 1540
  148.7 2.9 copy-start.7
  150.4 1.2 copy-start.3
  165.4 7.6 %copy-start.13 = (f32[2,4,4,4]{3,2,1,0:T(4,128)S(1)}, f32[2,4,4,4]{3,2,1,0:T(4,128)}, u32[]{:S(2)}) copy-start(f32[2,4,4,4]{3,2,1,0:T(4,128)} %param.12) | copy-start | bytes 1540
  202.6 368.5 %all-reduce.15.cloned.1.call-start = ((), (), s32[]{:S(2)}) async-start(), calls=%async_computation.5 | async-start | bytes 425984 | tf_op jit(solution)/shard_map/psum | solution.py:183
  204.0 100.6 %copy-start.16 = (f32[32]{0:T(128)S(1)}, f32[32]{0:T(128)}, u32[]{:S(2)}) copy-start(f32[32]{0:T(128)} %get-tuple-element.26) | copy-start | bytes 388
  204.0 103.0 %copy-start.12 = (f32[1024]{0:T(1024)S(1)}, f32[1024]{0:T(1024)}, u32[]{:S(2)}) copy-start(f32[1024]{0:T(1024)} %dynamic-update-slice) | copy-start | bytes 12292
  204.0 235.5 %copy-start.10 = (f32[1024]{0:T(1024)S(1)}, f32[1024]{0:T(1024)}, u32[]{:S(2)}) copy-start(f32[1024]{0:T(1024)} %copy-done.9) | copy-start | bytes 12292
  306.5 0.5 copy-start.18
  445.0 128.9 %all-gather.3.cloned.1.call-start = ((), (), s32[]{:S(2)}) async-start(), calls=%async_computation.1 | async-start | bytes 3514368 | tf_op jit(solution)/shard_map/all_gather | solution.py:193
  445.6 165.8 %all-gather.5.cloned.1.call-start = ((), (), s32[]{:S(2)}) async-start(), calls=%async_computation.4 | async-start | bytes 3514368 | tf_op jit(solution)/shard_map/all_gather | solution.py:192
  449.0 166.0 %all-to-all-start = ((bf16[32,32,1664]{2,1,0:T(8,128)(2,1)}), bf16[32,32,1664]{2,1,0:T(8,128)(2,1)}, u32[]{:S(2)}, u32[]{:S(2)}) async-start(bf16[32,32,1664]{2,1,0:T(8,128)(2,1)} %stack.8), calls=%async_computation | async-start | bytes 6815744 | tf_op jit(solution)/shard_map/all_to_all | solution.py:190
  459.7 5.2 copy-start.4
  460.6 110.4 %copy-start.6 = (bf16[32,1664]{1,0:T(8,128)(2,1)S(1)}, bf16[32,1664]{1,0:T(8,128)(2,1)}, u32[]{:S(2)}) copy-start(bf16[32,1664]{1,0:T(8,128)(2,1)} %param.9) | copy-start | bytes 319492
  460.6 110.4 %copy-start.15 = (f32[32]{0:T(128)S(1)}, f32[32]{0:T(128)}, u32[]{:S(2)}) copy-start(f32[32]{0:T(128)} %copy-done.14) | copy-start | bytes 388
  573.9 41.2 %copy-start.17 = (f32[1024]{0:T(1024)S(1)}, f32[1024]{0:T(1024)}, u32[]{:S(2)}) copy-start(f32[1024]{0:T(1024)} %get-tuple-element.21) | copy-start | bytes 12292
Sparse Core Ops, SparseCore 0:
  23.0 102.7 all-reduce.10
  202.7 101.8 all-reduce.12
  445.1 125.8 all-reduce.14
Sparse Core Ops, SparseCore 1:
  447.3 97.1 all-gather.2
  546.2 65.1 all-gather.4
